TPU v7x, 256 devices: a whole 4x4x8 slice. The times are simulated.
256 devices in a mesh: rows: 32 (over z, y_lo, core), chan: 8 (over x, y_hi).
Axes of the slice: x: 4, y: 4 (y_hi: 2, y_lo: 2; y = y_hi * 2 + y_lo), z: 8, core: 2. Of those that a mesh axis runs over, the one named last changes fastest.
Arguments:
- frame_one: bfloat16 [8192, 256], P('rows', 'chan'), may hold values from -6 to 6
- frame_two: bfloat16 [256, 480, 256], P('rows', None, 'chan'), may hold values from -6 to 6
Outputs:
- pyramid: bfloat16 [32, 5040, 8192], P(None, 'chan', 'rows')
All inputs are finite; a program needn't handle non-finite values.
Results may differ from a plain program's by a relative error of at most 0.0016.
Values may be sent and summed in bfloat16 or wider, within the bound.
A program may use at most 128 MiB of HBM per device.

v0:
```python
import jax
import jax.numpy as jnp
from jax import lax
from jax.sharding import PartitionSpec as P


def pool_strip(strip):
    full = strip.astype(jnp.float32)
    rows_n, cols_n, chans = full.shape
    level_one = full.reshape(rows_n // 2, 2, cols_n // 2, 2, chans).mean(axis=(1, 3))
    level_two = level_one.reshape(rows_n // 4, 2, cols_n // 4, 2, chans).mean(axis=(1, 3))
    joined = jnp.concatenate(
        [full.reshape(-1, chans), level_one.reshape(-1, chans), level_two.reshape(-1, chans)],
        axis=0,
    )
    return joined.astype(jnp.bfloat16)


def local(frame_one, frame_two):
    queries = lax.all_gather(frame_one, "chan", axis=1, tiled=True)
    channels = queries.shape[1]
    factor = 1.0 / jnp.sqrt(jnp.float32(channels))
    pooled = pool_strip(frame_two)
    strip_count = lax.axis_size("rows")
    groups = lax.axis_size("chan")
    share = pooled.shape[0] // groups
    slices = pooled.shape[1]
    arranged = jnp.transpose(pooled.reshape(groups, share, slices), (0, 2, 1))
    gathered = lax.all_gather(arranged, "rows", axis=1, tiled=True)
    traded = lax.all_to_all(gathered, "chan", split_axis=0, concat_axis=1, tiled=True)
    traded = traded.reshape(groups, strip_count, slices, share)
    split_queries = queries.reshape(queries.shape[0], groups, slices)
    values = jnp.einsum("kscp,qkc->spq", traded, split_queries, preferred_element_type=jnp.float32)
    return (values * factor).astype(jnp.bfloat16)


def solution(mesh):
    in_specs = (P("rows", "chan"), P("rows", None, "chan"))
    out_specs = P(None, "chan", "rows")
    return jax.shard_map(local, mesh=mesh, in_specs=in_specs, out_specs=out_specs, check_vma=False)
```

profile of v0, /device:TPU:32, one launch (start us, length us, event | category | flops | bytes accessed | tf_op | source)
XLA Modules:
  0.0 323.3 jit_solution(6841564967773849666)
XLA Ops:
  6.5 0.0 all-gather.2.cloned.1.call-start
  6.5 1.1 copy.14
  7.6 1.3 copy.15
  8.9 0.4 reshape.37
  9.3 1.6 reduce_sum.18
  10.9 0.1 broadcast_multiply_fusion
  11.0 0.4 reduce_sum.19
  11.4 0.1 copy.17
  11.5 0.1 copy.22
  11.6 0.1 concatenate.4
  11.7 1.2 convert_element_type.9
  12.9 0.0 all-gather.2.cloned.1.call-update
  12.9 77.1 %all-gather.2.cloned.1.call-done = bf16[8,1024,630]{2,0,1:T(8,128)(2,1)} async-done(((bf16[8,32,630]{2,0,1:T(8,128)(2,1)}), bf16[8,1024,630]{2,0,1:T(8,128)(2,1)}) %all-gather.2.cloned.1.call-update) | async-done | bytes 10321936 | tf_op jit(solution)/shard_map/all_gather | solution.py:29
  90.0 15.1 %copy.18 = bf16[8,1024,630]{1,2,0:T(8,128)(2,1)} copy(bf16[8,1024,630]{2,0,1:T(8,128)(2,1)} %all-gather.2.cloned.1.call-done) | data formatting | bytes 20643840 | tf_op jit(solution)/shard_map/all_gather | solution.py:29
  105.1 0.0 copy-start
  105.1 6.8 %all-to-all-start = ((bf16[8,1024,630]{1,2,0:T(8,128)(2,1)}), bf16[8,1024,630]{1,2,0:T(8,128)(2,1)}, u32[]{:S(2)}, u32[]{:S(2)}) async-start(bf16[8,1024,630]{1,2,0:T(8,128)(2,1)} %copy.18), calls=%async_computation | async-start | bytes 20709376 | tf_op jit(solution)/shard_map/all_to_all | solution.py:30
  112.0 0.0 copy-done
  112.0 168.7 %all_gather.7 = bf16[256,256]{0,1:T(8,128)(2,1)S(1)} all-gather(bf16[256,32]{0,1:T(8,128)(2,1)S(1)} %copy-done), channel_id=1, replica_groups=mesh['rows'=32,'chan'=8] {'chan'}, dimensions={1}, use_global_device_ids=true | all-gather | bytes 147456 | tf_op jit(solution)/shard_map/all_gather | solution.py:20
  280.6 0.0 all-to-all-done
  280.6 14.6 %copy.19 = bf16[8,1024,630]{2,1,0:T(8,128)(2,1)} copy(bf16[8,1024,630]{1,2,0:T(8,128)(2,1)} %all-to-all-done) | data formatting | bytes 20643840 | tf_op jit(solution)/shard_map/all_to_all | solution.py:30
  295.3 10.7 %fusion = bf16[32,630,256]{2,1,0:T(8,128)(2,1)} fusion(bf16[8,32,32,630]{3,2,1,0:T(8,128)(2,1)} %bitcast.21, bf16[256,8,32,1]{0,2,3,1:T(8,128)(2,1)S(1)} %bitcast.27), kind=kOutput, calls=%fused_computation.1 | convolution fusion | flops 2652733440 | bytes 20774912 | tf_op jit(solution)/shard_map/kscp,qkc->spq/dot_general | solution.py:33
  306.0 10.5 %copy.20 = bf16[32,630,256]{2,0,1:T(8,128)(2,1)} copy(bf16[32,630,256]{2,1,0:T(8,128)(2,1)} %fusion) | data formatting | bytes 20643840 | tf_op jit(solution)/shard_map/convert_element_type | solution.py:34
  (1 shorter events, 0.0 us)
Async XLA Ops:
  6.5 83.5 %all-gather.2.cloned.1.call-start = ((), (), s32[]{:S(2)}) async-start(), calls=%async_computation.1 | async-start | bytes 10813440 | tf_op jit(solution)/shard_map/all_gather | solution.py:29
  105.1 6.8 %copy-start = (bf16[256,32]{0,1:T(8,128)(2,1)S(1)}, bf16[256,32]{0,1:T(8,128)(2,1)}, u32[]{:S(2)}) copy-start(bf16[256,32]{0,1:T(8,128)(2,1)} %param.2) | copy-start | bytes 49156
  105.1 175.5 %all-to-all-start = ((bf16[8,1024,630]{1,2,0:T(8,128)(2,1)}), bf16[8,1024,630]{1,2,0:T(8,128)(2,1)}, u32[]{:S(2)}, u32[]{:S(2)}) async-start(bf16[8,1024,630]{1,2,0:T(8,128)(2,1)} %copy.18), calls=%async_computation | async-start | bytes 20709376 | tf_op jit(solution)/shard_map/all_to_all | solution.py:30
Sparse Core Ops, SparseCore 0:
  13.0 76.9 all-gather.1
where the time goes:
time: 324 us; the launch traced here: 323 us
  blocking collectives  169 us (52%)
  waiting for transfers between devices  77.1 us (24%)
  local copies, waits for them, and re-layouts  44.4 us (14%)
  between operations  13.4 us (4%)
  matrix products  10.7 us (3%)
  starting transfers between devices  6.84 us (2%)
    all_gather x1, blocking collectives, local(): queries = lax.all_gather(frame_one, 'chan', axis=1, tiled=True)  169 us
    all_gather x1, waiting for transfers between devices, local(): gathered = lax.all_gather(arranged, 'rows', axis=1, tiled=True)  77.1 us
    all_gather x1, local copies, waits for them, and re-layouts, local(): gathered = lax.all_gather(arranged, 'rows', axis=1, tiled=True)  15.1 us
    all_to_all x1, local copies, waits for them, and re-layouts, local(): lax.all_to_all(gathered, 'chan', split_axis=0, concat_axis=1, tiled=True)  14.6 us
    dot_general x1, matrix products, local(): jnp.einsum('kscp,qkc->spq', traded, split_queries, preferred_element_type...  10.7 us
    convert_element_type x1, local copies, waits for them, and re-layouts, local(): return (values * factor).astype(jnp.bfloat16)  10.5 us
    all_to_all x1, starting transfers between devices, local(): lax.all_to_all(gathered, 'chan', split_axis=0, concat_axis=1, tiled=True)  6.84 us
  transfers between devices with their start and end apart: 2, of which 1 were waited for; matrix products, arithmetic and copies ran while one was open for 0% of the time, Pallas kernels for 0%

commit v1 on v0

--- a/solution.py
+++ b/solution.py
@@ -2,6 +2,13 @@
 import jax.numpy as jnp
 from jax import lax
 from jax.sharding import PartitionSpec as P
+
+
+def exchange_gather(x, axis, d):
+    size = lax.axis_size(axis)
+    blocks = jnp.stack([x for _ in range(size)])
+    blocks = lax.all_to_all(blocks, axis, split_axis=0, concat_axis=0)
+    return jnp.concatenate(blocks, axis=d)
 
 
 def pool_strip(strip):
@@ -17,7 +24,7 @@
 
 
 def local(frame_one, frame_two):
-    queries = lax.all_gather(frame_one, "chan", axis=1, tiled=True)
+    queries = exchange_gather(frame_one, "chan", 1)
     channels = queries.shape[1]
     factor = 1.0 / jnp.sqrt(jnp.float32(channels))
     pooled = pool_strip(frame_two)

time: 324 us -> 278 us (0.86)
  blocking collectives: 169 us -> 124 us
  starting transfers between devices: 6.84 us -> 3.37 us
    all_gather x1 -> x0, blocking collectives: 169 us -> none  [local(): queries = lax.all_gather(frame_one, 'chan', axis=1, tiled=True)]
    all_to_all x0 -> x1, blocking collectives: none -> 124 us  [local(): lax.all_to_all(gathered, 'chan', split_axis=0, concat_axis=1, tiled=True)]
    all_to_all x1, starting transfers between devices: 6.84 us -> 3.37 us  [exchange_gather(): blocks = lax.all_to_all(blocks, axis, split_axis=0, concat_axis=0)]
  transfers between devices with their start and end apart: 2 -> 2, of which waited for: 1 -> 1; matrix products, arithmetic and copies ran while one was open for 0% -> 5% of each run, Pallas kernels for 0% -> 0%
where the time goes in v1:
time: 278 us; the launch traced here: 276 us
  blocking collectives  124 us (45%)
  waiting for transfers between devices  77.1 us (28%)
  local copies, waits for them, and re-layouts  45.1 us (16%)
  between operations  13.5 us (5%)
  matrix products  10.7 us (4%)
  starting transfers between devices  3.37 us (1%)
    all_to_all x1, blocking collectives, local(): lax.all_to_all(gathered, 'chan', split_axis=0, concat_axis=1, tiled=True)  124 us
    all_gather x1, waiting for transfers between devices, local(): gathered = lax.all_gather(arranged, 'rows', axis=1, tiled=True)  77.1 us
    all_gather x1, local copies, waits for them, and re-layouts, local(): gathered = lax.all_gather(arranged, 'rows', axis=1, tiled=True)  15.1 us
    all_to_all x1, local copies, waits for them, and re-layouts, local(): lax.all_to_all(gathered, 'chan', split_axis=0, concat_axis=1, tiled=True)  14.6 us
    dot_general x1, matrix products, local(): jnp.einsum('kscp,qkc->spq', traded, split_queries, preferred_element_type...  10.7 us
    convert_element_type x1, local copies, waits for them, and re-layouts, local(): return (values * factor).astype(jnp.bfloat16)  10.5 us
  transfers between devices with their start and end apart: 2, of which 1 were waited for; matrix products, arithmetic and copies ran while one was open for 5% of the time, Pallas kernels for 0%

profile of v1, /device:TPU:32, one launch (start us, length us, event | category | flops | bytes accessed | tf_op | source)
XLA Modules:
  0.0 276.0 jit_solution(12364200053475712282)
XLA Ops:
  6.5 0.0 all-gather.2.cloned.1.call-start
  6.5 1.1 copy.14
  7.6 1.3 copy.15
  8.9 0.4 reshape.39
  9.3 1.6 reduce_sum.18
  10.9 0.1 broadcast_multiply_fusion
  11.0 0.4 reduce_sum.19
  11.4 0.1 copy.17
  11.5 0.1 copy.22
  11.6 0.1 concatenate.4
  11.7 1.2 convert_element_type.9
  12.9 0.0 all-gather.2.cloned.1.call-update
  12.9 77.1 %all-gather.2.cloned.1.call-done = bf16[8,1024,630]{2,0,1:T(8,128)(2,1)} async-done(((bf16[8,32,630]{2,0,1:T(8,128)(2,1)}), bf16[8,1024,630]{2,0,1:T(8,128)(2,1)}) %all-gather.2.cloned.1.call-update) | async-done | bytes 10321936 | tf_op jit(solution)/shard_map/all_gather | solution.py:36
  90.0 15.1 %copy.18 = bf16[8,1024,630]{1,2,0:T(8,128)(2,1)} copy(bf16[8,1024,630]{2,0,1:T(8,128)(2,1)} %all-gather.2.cloned.1.call-done) | data formatting | bytes 20643840 | tf_op jit(solution)/shard_map/all_gather | solution.py:36
  105.1 0.0 copy-start
  105.1 124.1 %all_to_all.14 = bf16[8,1024,630]{1,2,0:T(8,128)(2,1)} all-to-all(bf16[8,1024,630]{1,2,0:T(8,128)(2,1)} %copy.18), channel_id=1, replica_groups=mesh['rows'=32,'chan'=8] {'chan'}, dimensions={0} | all-to-all | bytes 20643840 | tf_op jit(solution)/shard_map/all_to_all | solution.py:37
  229.2 0.0 copy-done
  229.2 0.7 stack.2
  229.9 3.4 %all-to-all-start.1 = ((bf16[8,256,32]{1,2,0:T(8,128)(2,1)}), bf16[8,256,32]{1,2,0:T(8,128)(2,1)S(1)}, u32[]{:S(2)}, u32[]{:S(2)}) async-start(bf16[8,256,32]{1,2,0:T(8,128)(2,1)} %stack.2), calls=%async_computation.1 | async-start | bytes 262144 | tf_op jit(solution)/shard_map/all_to_all | solution.py:10
  233.3 14.6 %copy.19 = bf16[8,1024,630]{2,1,0:T(8,128)(2,1)} copy(bf16[8,1024,630]{1,2,0:T(8,128)(2,1)} %all_to_all.14) | data formatting | bytes 20643840 | tf_op jit(solution)/shard_map/all_to_all | solution.py:37
  247.9 0.0 all-to-all-done.1
  247.9 10.7 %fusion = bf16[32,630,256]{2,1,0:T(8,128)(2,1)} fusion(bf16[8,32,32,630]{3,2,1,0:T(8,128)(2,1)} %bitcast.22, bf16[8,256,32]{1,2,0:T(8,128)(2,1)S(1)} %all-to-all-done.1), kind=kOutput, calls=%fused_computation.1 | convolution fusion | flops 2652733440 | bytes 20774912 | tf_op jit(solution)/shard_map/kscp,qkc->spq/dot_general | solution.py:40
  258.6 10.5 %copy.20 = bf16[32,630,256]{2,0,1:T(8,128)(2,1)} copy(bf16[32,630,256]{2,1,0:T(8,128)(2,1)} %fusion) | data formatting | bytes 20643840 | tf_op jit(solution)/shard_map/convert_element_type | solution.py:41
  (1 shorter events, 0.0 us)
Async XLA Ops:
  6.5 83.5 %all-gather.2.cloned.1.call-start = ((), (), s32[]{:S(2)}) async-start(), calls=%async_computation.2 | async-start | bytes 10813440 | tf_op jit(solution)/shard_map/all_gather | solution.py:36
  105.1 124.1 %copy-start = (bf16[256,32]{0,1:T(8,128)(2,1)S(1)}, bf16[256,32]{0,1:T(8,128)(2,1)}, u32[]{:S(2)}) copy-start(bf16[256,32]{0,1:T(8,128)(2,1)} %param.2) | copy-start | bytes 49156
  229.9 18.0 %all-to-all-start.1 = ((bf16[8,256,32]{1,2,0:T(8,128)(2,1)}), bf16[8,256,32]{1,2,0:T(8,128)(2,1)S(1)}, u32[]{:S(2)}, u32[]{:S(2)}) async-start(bf16[8,256,32]{1,2,0:T(8,128)(2,1)} %stack.2), calls=%async_computation.1 | async-start | bytes 262144 | tf_op jit(solution)/shard_map/all_to_all | solution.py:10
Sparse Core Ops, SparseCore 0:
  13.0 76.9 all-gather.1
